TPU v7x, 128 devices: a whole 4x4x4 slice. The times are simulated.
128 devices in a mesh: cell: 16 (over x, z_hi, core), tm: 8 (over y, z_lo).
Axes of the slice: x: 4, y: 4, z: 4 (z_hi: 2, z_lo: 2; z = z_hi * 2 + z_lo), core: 2. Of those that a mesh axis runs over, the one named last changes fastest.
Arguments:
- window: float32 [16384, 16384], P('cell', 'tm'), may hold values from -0.09375 to 0.09375
- range_test: float32 [16384, 256], P('tm'), may hold values from -0.046875 to 0.046875
- co_test: float32 [256, 16384], P(None, 'cell'), may hold values from -0.046875 to 0.046875
- core_left: float32 [512, 16384], P(None, 'cell'), may hold values from -0.046875 to 0.046875
- core_right: float32 [512, 16384], P(None, 'tm'), may hold values from -0.046875 to 0.046875
Outputs:
- range_basis: float32 [16384, 256], P('cell')
- co_basis: float32 [256, 16384], P(None, 'tm')
- core: float32 [256, 256], replicated
All inputs are finite; a program needn't handle non-finite values.
Results may differ from a plain program's by a relative error of at most 0.00023.
Values sent between devices are 32-bit elements; how exact they have to be, the bound alone decides.
A program may use at most 128 MiB of HBM per device.

v0:
```python
import math
import jax
import jax.numpy as jnp
from jax import lax
from jax.sharding import PartitionSpec as P


def inner_rows(left, right):
    return lax.dot_general(left, right, (((0,), (0,)), ((), ())), precision=lax.Precision.HIGHEST)


def inner_cols(left, right):
    return lax.dot_general(left, right, (((1,), (1,)), ((), ())), precision=lax.Precision.HIGHEST)


def product(left, right):
    return jnp.dot(left, right, precision=lax.Precision.HIGHEST, preferred_element_type=jnp.float32)


def per_device(window, range_test, co_test, core_left, core_right):
    rows_total = window.shape[0] * lax.axis_size("cell")
    cols_total = window.shape[1] * lax.axis_size("tm")
    range_term = product(window, range_test)
    co_term = product(co_test, window)
    left_window = product(core_left, window)
    core_term = inner_cols(left_window, core_right)
    sketch_z = lax.psum(core_term, ("cell", "tm"))
    range_full = lax.psum(range_term, "tm")
    co_full = lax.psum(co_term, "cell")
    gram_y = lax.psum(inner_rows(range_full, range_full) / rows_total, "cell")
    gram_w = lax.psum(inner_cols(co_full, co_full) / cols_total, "tm")
    lower_y = jnp.linalg.cholesky(gram_y)
    lower_w = jnp.linalg.cholesky(gram_w)
    range_basis = jax.scipy.linalg.solve_triangular(lower_y, range_full.T, lower=True).T
    co_basis = jax.scipy.linalg.solve_triangular(lower_w, co_full, lower=True)
    left_image = lax.psum(product(core_left, range_basis), "cell")
    right_image = lax.psum(inner_cols(core_right, co_basis), "tm")
    gram_left = inner_rows(left_image, left_image)
    gram_right = inner_rows(right_image, right_image)
    projected = inner_rows(left_image, sketch_z)
    left_solved = jax.scipy.linalg.cho_solve((jnp.linalg.cholesky(gram_left), True), projected)
    middle = product(left_solved, right_image)
    core = jax.scipy.linalg.cho_solve((jnp.linalg.cholesky(gram_right), True), middle.T).T
    core = core * math.sqrt(rows_total * cols_total)
    return (range_basis, co_basis, core)


def solution(mesh):
    return jax.shard_map(
        per_device,
        mesh=mesh,
        in_specs=(P("cell", "tm"), P("tm", None), P(None, "cell"), P(None, "cell"), P(None, "tm")),
        out_specs=(P("cell", None), P(None, "tm"), P()),
        check_vma=False,
    )
```

profile of v0, /device:TPU:0, one launch (start us, length us, event | category | flops | bytes accessed | tf_op | source)
XLA Modules:
  0.0 920.8 jit_solution(13198876106782574047)
XLA Ops:
  7.2 10.7 %fusion.50 = f32[1024,256]{1,0:T(8,128)} fusion(f32[1024,2048]{1,0:T(8,128)} %param.6, f32[2048,256]{1,0:T(8,128)} %param.7), kind=kOutput, calls=%fused_computation.123 | convolution fusion | flops 6442450944 | bytes 11534336 | tf_op jit(solution)/shard_map/dot_general | solution.py:17
  18.0 80.7 %all-reduce.9.cloned.1.call-done = f32[1024,256]{1,0:T(8,128)} async-done(((f32[1024,256]{1,0:T(8,128)}), f32[1024,256]{1,0:T(8,128)}) %all-reduce.9.cloned.1.call-update) | async-done | bytes 1048592 | tf_op jit(solution)/shard_map/psum | solution.py:28
  98.6 4.1 convolution_multiply_fusion.1
  102.8 10.7 %fusion.51 = f32[256,2048]{1,0:T(8,128)} fusion(f32[256,1024]{1,0:T(8,128)S(1)} %copy-done.12, f32[1024,2048]{1,0:T(8,128)} %param.6), kind=kOutput, calls=%fused_computation.124 | convolution fusion | flops 6442450944 | bytes 11534336 | tf_op jit(solution)/shard_map/dot_general | solution.py:17
  113.5 127.4 %all-reduce.11.cloned.1.call-done = f32[256,256]{0,1:T(8,128)} async-done(((f32[256,256]{0,1:T(8,128)}), f32[256,256]{0,1:T(8,128)}) %all-reduce.11.cloned.1.call-update) | async-done | bytes 262160 | tf_op jit(solution)/shard_map/psum | solution.py:30
  243.7 11.7 %cholesky.214 = f32[128,128]{1,0:T(8,128)S(1)} custom-call(f32[128,128]{1,0:T(8,128)S(1)} %cholesky.346), custom_call_target="Cholesky" | custom-call | tf_op jit(solution)/shard_map/jit(cholesky)/cholesky | solution.py:32
  255.5 9.8 %custom-call.37 = f32[1,128,128]{1,2,0:T(8,128)S(1)} custom-call(f32[1,128,128]{2,1,0:T(8,128)S(1)} %get-tuple-element.96), custom_call_target="InvertDiagBlocksLowerTriangular" | custom-call | tf_op jit(solution)/shard_map/jit(cholesky)/cholesky | solution.py:32
  267.4 11.7 %cholesky.231 = f32[128,128]{1,0:T(8,128)S(1)} custom-call(f32[128,128]{1,0:T(8,128)S(1)} %convolution_subtract_fusion.9), custom_call_target="Cholesky" | custom-call | tf_op jit(solution)/shard_map/jit(cholesky)/cholesky | solution.py:32
  282.3 4.1 while.4
  287.0 20.7 %custom-call.30 = f32[2,128,128]{1,2,0:T(8,128)S(1)} custom-call(f32[2,128,128]{2,1,0:T(8,128)} %copy-done.17), custom_call_target="InvertDiagBlocksLowerTriangular" | custom-call | tf_op jit(solution)/shard_map/jit(_solve_triangular)/triangular_solve | solution.py:34
  312.9 16.9 %fusion.54 = f32[512,2048]{1,0:T(8,128)S(1)} fusion(f32[512,1024]{1,0:T(8,128)S(1)} %copy-done, f32[1024,2048]{1,0:T(8,128)} %param.6), kind=kOutput, calls=%fused_computation.127 | convolution fusion | flops 12884901888 | bytes 14680064 | tf_op jit(solution)/shard_map/dot_general | solution.py:17
  329.8 7.9 fusion.55
  344.1 116.8 %all-reduce.19.cloned.1.call-done = (f32[256,2048]{1,0:T(8,128)}, f32[512,256]{0,1:T(8,128)}) async-done(((f32[256,2048]{1,0:T(8,128)}, f32[512,256]{0,1:T(8,128)}), (f32[256,2048]{1,0:T(8,128)}, f32[512,256]{0,1:T(8,128)})) %all-reduce.19.cloned.1.call-update) | async-done | bytes 2621456 | tf_op jit(solution)/shard_map/psum | solution.py:29
  462.9 11.7 %cholesky.316 = f32[128,128]{1,0:T(8,128)S(1)} custom-call(f32[128,128]{1,0:T(8,128)S(1)} %cholesky.355), custom_call_target="Cholesky" | custom-call | tf_op jit(solution)/shard_map/jit(cholesky)/cholesky | solution.py:41
  474.7 9.8 %custom-call.40 = f32[1,128,128]{1,2,0:T(8,128)S(1)} custom-call(f32[1,128,128]{2,1,0:T(8,128)S(1)} %get-tuple-element.88), custom_call_target="InvertDiagBlocksLowerTriangular" | custom-call | tf_op jit(solution)/shard_map/jit(cholesky)/cholesky | solution.py:41
  485.0 11.7 %cholesky.333 = f32[128,128]{1,0:T(8,128)S(1)} custom-call(f32[128,128]{1,0:T(8,128)S(1)} %convolution_subtract_fusion.6), custom_call_target="Cholesky" | custom-call | tf_op jit(solution)/shard_map/jit(cholesky)/cholesky | solution.py:41
  499.5 4.1 while.7
  503.6 19.7 %custom-call.33 = f32[2,128,128]{1,2,0:T(8,128)S(1)} custom-call(f32[2,128,128]{2,1,0:T(8,128)S(1)} %get-tuple-element.35), custom_call_target="InvertDiagBlocksLowerTriangular" | custom-call | tf_op jit(solution)/shard_map/jit(_cho_solve)/triangular_solve | solution.py:41
  523.3 4.8 convolution_multiply_fusion
  528.6 85.9 %all-reduce.17.cloned.1.call-done = f32[512,512]{1,0:T(8,128)} async-done(((f32[512,512]{1,0:T(8,128)}), f32[512,512]{1,0:T(8,128)}) %all-reduce.17.cloned.1.call-update) | async-done | bytes 1048592 | tf_op jit(solution)/shard_map/psum | solution.py:27
  618.1 73.0 %all-reduce.13.cloned.1.call-done = f32[256,256]{0,1:T(8,128)} async-done(((f32[256,256]{0,1:T(8,128)}), f32[256,256]{0,1:T(8,128)}) %all-reduce.13.cloned.1.call-update) | async-done | bytes 262160 | tf_op jit(solution)/shard_map/psum | solution.py:31
  693.2 11.7 %cholesky.248 = f32[128,128]{1,0:T(8,128)S(1)} custom-call(f32[128,128]{1,0:T(8,128)S(1)} %cholesky.349), custom_call_target="Cholesky" | custom-call | tf_op jit(solution)/shard_map/jit(cholesky)/cholesky | solution.py:33
  705.0 9.8 %custom-call.38 = f32[1,128,128]{1,2,0:T(8,128)S(1)} custom-call(f32[1,128,128]{2,1,0:T(8,128)S(1)} %get-tuple-element.92), custom_call_target="InvertDiagBlocksLowerTriangular" | custom-call | tf_op jit(solution)/shard_map/jit(cholesky)/cholesky | solution.py:33
  716.9 11.9 %cholesky.265 = f32[128,128]{1,0:T(8,128)S(1)} custom-call(f32[128,128]{1,0:T(8,128)S(1)} %convolution_subtract_fusion.8), custom_call_target="Cholesky" | custom-call | tf_op jit(solution)/shard_map/jit(cholesky)/cholesky | solution.py:33
  735.5 19.7 %custom-call.31 = f32[2,128,128]{1,2,0:T(8,128)S(1)} custom-call(f32[2,128,128]{2,1,0:T(8,128)S(1)} %get-tuple-element.19), custom_call_target="InvertDiagBlocksLowerTriangular" | custom-call | tf_op jit(solution)/shard_map/jit(_solve_triangular)/triangular_solve | solution.py:35
  762.6 4.5 convolution_bitcast_fusion.1
  768.3 73.2 %all-reduce.15.cloned.1.call-done = f32[512,256]{0,1:T(8,128)} async-done(((f32[512,256]{0,1:T(8,128)}), f32[512,256]{0,1:T(8,128)}) %all-reduce.15.cloned.1.call-update) | async-done | bytes 524304 | tf_op jit(solution)/shard_map/psum | solution.py:37
  845.9 11.9 %cholesky.282 = f32[128,128]{1,0:T(8,128)S(1)} custom-call(f32[128,128]{1,0:T(8,128)S(1)} %cholesky.352), custom_call_target="Cholesky" | custom-call | tf_op jit(solution)/shard_map/jit(cholesky)/cholesky | solution.py:43
  857.8 9.8 %custom-call.39 = f32[1,128,128]{1,2,0:T(8,128)S(1)} custom-call(f32[1,128,128]{2,1,0:T(8,128)S(1)} %get-tuple-element.84), custom_call_target="InvertDiagBlocksLowerTriangular" | custom-call | tf_op jit(solution)/shard_map/jit(cholesky)/cholesky | solution.py:43
  869.8 11.7 %cholesky.299 = f32[128,128]{1,0:T(8,128)S(1)} custom-call(f32[128,128]{1,0:T(8,128)S(1)} %convolution_subtract_fusion.7), custom_call_target="Cholesky" | custom-call | tf_op jit(solution)/shard_map/jit(cholesky)/cholesky | solution.py:43
  885.2 4.1 while.6
  890.0 20.5 %custom-call.32 = f32[2,128,128]{1,2,0:T(8,128)S(1)} custom-call(f32[2,128,128]{2,1,0:T(8,128)} %copy-done.16), custom_call_target="InvertDiagBlocksLowerTriangular" | custom-call | tf_op jit(solution)/shard_map/jit(_cho_solve)/triangular_solve | solution.py:43
  (150 shorter events, 74.1 us)
Async XLA Ops:
  7.2 302.9 %copy-start = (f32[512,1024]{1,0:T(8,128)S(1)}, f32[512,1024]{1,0:T(8,128)}, u32[]{:S(2)}) copy-start(f32[512,1024]{1,0:T(8,128)} %param.9) | copy-start | bytes 6291460
  7.2 91.5 %all-reduce.9.cloned.1.call-start = ((), (), s32[]{:S(2)}) async-start(), calls=%async_computation | async-start | bytes 2097152 | tf_op jit(solution)/shard_map/psum | solution.py:28
  17.9 84.9 %copy-start.12 = (f32[256,1024]{1,0:T(8,128)S(1)}, f32[256,1024]{1,0:T(8,128)}, u32[]{:S(2)}) copy-start(f32[256,1024]{1,0:T(8,128)} %param.8) | copy-start | bytes 3145732
  17.9 223.0 %all-reduce.11.cloned.1.call-start = ((), (), s32[]{:S(2)}) async-start(), calls=%async_computation.1 | async-start | bytes 524288 | tf_op jit(solution)/shard_map/psum | solution.py:30
  102.7 358.2 %all-reduce.19.cloned.1.call-start = ((), (), s32[]{:S(2)}) async-start(), calls=%async_computation.5 | async-start | bytes 5242880 | tf_op jit(solution)/shard_map/psum | solution.py:29
  113.5 194.2 %copy-start.4 = (f32[1024,256]{1,0:T(8,128)S(1)}, f32[1024,256]{1,0:T(8,128)}, u32[]{:S(2)}) copy-start(f32[1024,256]{1,0:T(8,128)} %all-reduce.9.cloned.1.call-done) | copy-start | bytes 3145732
  243.0 0.7 copy-start.13
  279.2 2.0 copy-start.10
  286.4 0.7 copy-start.17
  308.4 1.7 copy-start.5
  312.8 301.7 %all-reduce.17.cloned.1.call-start = ((), (), s32[]{:S(2)}) async-start(), calls=%async_computation.4 | async-start | bytes 2097152 | tf_op jit(solution)/shard_map/psum | solution.py:27
  312.9 16.9 %copy-start.2 = (f32[512,2048]{1,0:T(8,128)S(1)}, f32[512,2048]{1,0:T(8,128)}, u32[]{:S(2)}) copy-start(f32[512,2048]{1,0:T(8,128)} %param.10) | copy-start | bytes 12582916
  329.8 10.7 %copy-start.6 = (f32[128,1024]{1,0:T(8,128)S(1)}, f32[128,1024]{1,0:T(8,128)}, u32[]{:S(2)}) copy-start(f32[128,1024]{1,0:T(8,128)} %copy-done.5) | copy-start | bytes 1572868
  337.7 353.3 %all-reduce.13.cloned.1.call-start = ((), (), s32[]{:S(2)}) async-start(), calls=%async_computation.2 | async-start | bytes 524288 | tf_op jit(solution)/shard_map/psum | solution.py:31
  523.3 91.3 %copy-start.9 = (f32[512,256]{0,1:T(8,128)S(1)}, f32[512,256]{0,1:T(8,128)}, u32[]{:S(2)}) copy-start(f32[512,256]{0,1:T(8,128)} %get-tuple-element.72) | copy-start | bytes 1572868
  528.2 313.4 %all-reduce.15.cloned.1.call-start = ((), (), s32[]{:S(2)}) async-start(), calls=%async_computation.3 | async-start | bytes 1048576 | tf_op jit(solution)/shard_map/psum | solution.py:37
  693.2 11.7 %copy-start.14 = (f32[256,256]{1,0:T(8,128)}, f32[256,256]{1,0:T(8,128)S(1)}, u32[]{:S(2)}) copy-start(f32[256,256]{1,0:T(8,128)S(1)} %fusion.14) | copy-start | bytes 786436
  755.2 2.4 copy-start.1
  759.7 2.9 copy-start.3
  759.9 1.3 copy-start.7
  843.3 67.1 %copy-start.8 = (f32[512,256]{0,1:T(8,128)S(1)}, f32[512,256]{0,1:T(8,128)}, u32[]{:S(2)}) copy-start(f32[512,256]{0,1:T(8,128)} %all-reduce.15.cloned.1.call-done) | copy-start | bytes 1572868
  845.2 0.7 copy-start.15
  882.3 1.9 copy-start.11
  889.3 0.7 copy-start.16
Sparse Core Ops, SparseCore 0:
  18.1 80.5 all-reduce.8
  102.8 138.0 all-reduce.10
  313.0 147.9 all-reduce.18
  465.6 148.9 all-reduce.16
  617.4 73.6 all-reduce.12
  767.3 74.1 all-reduce.14
where the time goes:
time: 929 us; the launch traced here: 921 us
  waiting for transfers between devices  557 us (60%)
  other arithmetic  225 us (24%)
  matrix products  86.6 us (9%)
  local copies, waits for them, and re-layouts  28.3 us (3%)
  between operations  20.2 us (2%)
    psum x1, waiting for transfers between devices, per_device(): gram_y = lax.psum(inner_rows(range_full, range_full) / rows_total, 'cell')  127 us
    psum x1, waiting for transfers between devices, per_device(): co_full = lax.psum(co_term, 'cell')  117 us
    psum x1, waiting for transfers between devices, per_device(): sketch_z = lax.psum(core_term, ('cell', 'tm'))  85.9 us
    psum x1, waiting for transfers between devices, per_device(): range_full = lax.psum(range_term, 'tm')  80.7 us
    psum x1, waiting for transfers between devices, per_device(): right_image = lax.psum(inner_cols(core_right, co_basis), 'tm')  73.2 us
    psum x1, waiting for transfers between devices, per_device(): gram_w = lax.psum(inner_cols(co_full, co_full) / cols_total, 'tm')  73 us
    dot_general x5, matrix products, product(): jnp.dot(left, right, precision=lax.Precision.HIGHEST, preferred_element_t...  41.6 us
    another operation x7, other arithmetic, per_device(): jnp.linalg.cholesky(gram_right)  34.8 us
  transfers between devices with their start and end apart: 6, of which 6 were waited for; matrix products, arithmetic and copies ran while one was open for 12% of the time, Pallas kernels for 0%

commit v1 on v0

--- a/solution.py
+++ b/solution.py
@@ -24,7 +24,7 @@
     co_term = product(co_test, window)
     left_window = product(core_left, window)
     core_term = inner_cols(left_window, core_right)
-    sketch_z = lax.psum(core_term, ("cell", "tm"))
+    sketch_z = lax.psum(lax.psum(core_term, "tm"), "cell")
     range_full = lax.psum(range_term, "tm")
     co_full = lax.psum(co_term, "cell")
     gram_y = lax.psum(inner_rows(range_full, range_full) / rows_total, "cell")

time: 929 us -> 832 us (0.90)
  waiting for transfers between devices: 557 us -> 467 us
    psum x1 -> x0, waiting for transfers between devices: 85.9 us -> none  [per_device(): sketch_z = lax.psum(core_term, ('cell', 'tm'))]
    psum x1, waiting for transfers between devices: 73 us -> 10.3 us  [per_device(): gram_w = lax.psum(inner_cols(co_full, co_full) / cols_total, 'tm')]
    psum x1, waiting for transfers between devices: 117 us -> 148 us  [per_device(): co_full = lax.psum(co_term, 'cell')]
    psum x1, waiting for transfers between devices: 80.7 us -> 107 us  [per_device(): range_full = lax.psum(range_term, 'tm')]
  transfers between devices with their start and end apart: 6 -> 5, of which waited for: 6 -> 5; matrix products, arithmetic and copies ran while one was open for 12% -> 10% of each run, Pallas kernels for 0% -> 0%
where the time goes in v1:
time: 832 us; the launch traced here: 826 us
  waiting for transfers between devices  467 us (56%)
  other arithmetic  226 us (27%)
  matrix products  82.3 us (10%)
  local copies, waits for them, and re-layouts  30.5 us (4%)
  between operations  19.7 us (2%)
    psum x1, waiting for transfers between devices, per_device(): co_full = lax.psum(co_term, 'cell')  148 us
    psum x1, waiting for transfers between devices, per_device(): gram_y = lax.psum(inner_rows(range_full, range_full) / rows_total, 'cell')  129 us
    psum x1, waiting for transfers between devices, per_device(): range_full = lax.psum(range_term, 'tm')  107 us
    psum x1, waiting for transfers between devices, per_device(): right_image = lax.psum(inner_cols(core_right, co_basis), 'tm')  73 us
    dot_general x5, matrix products, product(): jnp.dot(left, right, precision=lax.Precision.HIGHEST, preferred_element_t...  38.4 us
    another operation x7, other arithmetic, per_device(): jnp.linalg.cholesky(gram_right)  34.8 us
    another operation x7, other arithmetic, per_device(): lower_w = jnp.linalg.cholesky(gram_w)  34.7 us
    another operation x7, other arithmetic, per_device(): jnp.linalg.cholesky(gram_left)  34.6 us
  transfers between devices with their start and end apart: 5, of which 5 were waited for; matrix products, arithmetic and copies ran while one was open for 10% of the time, Pallas kernels for 0%

profile of v1, /device:TPU:0, one launch (start us, length us, event | category | flops | bytes accessed | tf_op | source)
XLA Modules:
  0.0 825.9 jit_solution(2092319959878946442)
XLA Ops:
  8.8 16.6 %fusion.54 = f32[512,2048]{1,0:T(8,128)S(1)} fusion(f32[512,1024]{1,0:T(8,128)S(1)} %copy-done, f32[1024,2048]{1,0:T(8,128)} %param.6), kind=kOutput, calls=%fused_computation.127 | convolution fusion | flops 12884901888 | bytes 14680064 | tf_op jit(solution)/shard_map/dot_general | solution.py:17
  25.4 7.6 fusion.50
  33.1 8.1 fusion.55
  41.2 106.8 %all-reduce.17.cloned.1.call-done = (f32[1024,256]{1,0:T(8,128)}, f32[512,512]{1,0:T(8,128)}) async-done(((f32[1024,256]{1,0:T(8,128)}, f32[512,512]{1,0:T(8,128)}), (f32[1024,256]{1,0:T(8,128)}, f32[512,512]{1,0:T(8,128)})) %all-reduce.17.cloned.1.call-update) | async-done | bytes 2097168 | tf_op jit(solution)/shard_map/psum | solution.py:28
  148.0 4.1 convolution_multiply_fusion.1
  152.2 10.7 %fusion.51 = f32[256,2048]{1,0:T(8,128)} fusion(f32[256,1024]{1,0:T(8,128)S(1)} %copy-done.14, f32[1024,2048]{1,0:T(8,128)} %param.6), kind=kOutput, calls=%fused_computation.124 | convolution fusion | flops 6442450944 | bytes 11534336 | tf_op jit(solution)/shard_map/dot_general | solution.py:17
  162.9 129.4 %all-reduce.9.cloned.1.call-done = f32[256,256]{0,1:T(8,128)} async-done(((f32[256,256]{0,1:T(8,128)}), f32[256,256]{0,1:T(8,128)}) %all-reduce.9.cloned.1.call-update) | async-done | bytes 262160 | tf_op jit(solution)/shard_map/psum | solution.py:30
  295.1 11.7 %cholesky.214 = f32[128,128]{1,0:T(8,128)S(1)} custom-call(f32[128,128]{1,0:T(8,128)S(1)} %cholesky.346), custom_call_target="Cholesky" | custom-call | tf_op jit(solution)/shard_map/jit(cholesky)/cholesky | solution.py:32
  306.8 9.8 %custom-call.37 = f32[1,128,128]{1,2,0:T(8,128)S(1)} custom-call(f32[1,128,128]{2,1,0:T(8,128)S(1)} %get-tuple-element.99), custom_call_target="InvertDiagBlocksLowerTriangular" | custom-call | tf_op jit(solution)/shard_map/jit(cholesky)/cholesky | solution.py:32
  318.8 11.7 %cholesky.231 = f32[128,128]{1,0:T(8,128)S(1)} custom-call(f32[128,128]{1,0:T(8,128)S(1)} %convolution_subtract_fusion.9), custom_call_target="Cholesky" | custom-call | tf_op jit(solution)/shard_map/jit(cholesky)/cholesky | solution.py:32
  333.6 4.1 while.4
  338.4 20.9 %custom-call.30 = f32[2,128,128]{1,2,0:T(8,128)S(1)} custom-call(f32[2,128,128]{2,1,0:T(8,128)} %copy-done.19), custom_call_target="InvertDiagBlocksLowerTriangular" | custom-call | tf_op jit(solution)/shard_map/jit(_solve_triangular)/triangular_solve | solution.py:34
  369.0 147.7 %all-reduce.15.cloned.1.call-done = (f32[256,2048]{1,0:T(8,128)}, f32[512,256]{0,1:T(8,128)}, f32[512,512]{1,0:T(8,128)}) async-done(((f32[256,2048]{1,0:T(8,128)}, f32[512,256]{0,1:T(8,128)}, f32[512,512]{1,0:T(8,128)}), (f32[256,2048]{1,0:T(8,128)}, f32[512,256]{0,1:T(8,128)}, f32[512,512]{1,0:T(8,128)})) %all-reduce.15.cloned.1.call-update) | async-done | bytes 3670032 | tf_op jit(solution)/shard_map/psum | solution.py:29
  516.7 4.8 convolution_multiply_fusion
  522.6 11.7 %cholesky.316 = f32[128,128]{1,0:T(8,128)S(1)} custom-call(f32[128,128]{1,0:T(8,128)S(1)} %cholesky.355), custom_call_target="Cholesky" | custom-call | tf_op jit(solution)/shard_map/jit(cholesky)/cholesky | solution.py:41
  534.4 9.8 %custom-call.40 = f32[1,128,128]{1,2,0:T(8,128)S(1)} custom-call(f32[1,128,128]{2,1,0:T(8,128)S(1)} %get-tuple-element.91), custom_call_target="InvertDiagBlocksLowerTriangular" | custom-call | tf_op jit(solution)/shard_map/jit(cholesky)/cholesky | solution.py:41
  544.7 11.7 %cholesky.333 = f32[128,128]{1,0:T(8,128)S(1)} custom-call(f32[128,128]{1,0:T(8,128)S(1)} %convolution_subtract_fusion.6), custom_call_target="Cholesky" | custom-call | tf_op jit(solution)/shard_map/jit(cholesky)/cholesky | solution.py:41
  559.0 3.8 while.7
  562.8 20.1 %custom-call.33 = f32[2,128,128]{1,2,0:T(8,128)S(1)} custom-call(f32[2,128,128]{2,1,0:T(8,128)S(1)} %get-tuple-element.35), custom_call_target="InvertDiagBlocksLowerTriangular" | custom-call | tf_op jit(solution)/shard_map/jit(_cho_solve)/triangular_solve | solution.py:41
  586.4 10.3 %all-reduce.11.cloned.1.call-done = f32[256,256]{0,1:T(8,128)} async-done(((f32[256,256]{0,1:T(8,128)}), f32[256,256]{0,1:T(8,128)}) %all-reduce.11.cloned.1.call-update) | async-done | bytes 262160 | tf_op jit(solution)/shard_map/psum | solution.py:31
  598.8 11.7 %cholesky.248 = f32[128,128]{1,0:T(8,128)S(1)} custom-call(f32[128,128]{1,0:T(8,128)S(1)} %cholesky.349), custom_call_target="Cholesky" | custom-call | tf_op jit(solution)/shard_map/jit(cholesky)/cholesky | solution.py:33
  610.6 9.8 %custom-call.38 = f32[1,128,128]{1,2,0:T(8,128)S(1)} custom-call(f32[1,128,128]{2,1,0:T(8,128)S(1)} %get-tuple-element.95), custom_call_target="InvertDiagBlocksLowerTriangular" | custom-call | tf_op jit(solution)/shard_map/jit(cholesky)/cholesky | solution.py:33
  622.5 11.7 %cholesky.265 = f32[128,128]{1,0:T(8,128)S(1)} custom-call(f32[128,128]{1,0:T(8,128)S(1)} %convolution_subtract_fusion.8), custom_call_target="Cholesky" | custom-call | tf_op jit(solution)/shard_map/jit(cholesky)/cholesky | solution.py:33
  637.1 4.0 while.5
  641.1 19.7 %custom-call.31 = f32[2,128,128]{1,2,0:T(8,128)S(1)} custom-call(f32[2,128,128]{2,1,0:T(8,128)S(1)} %get-tuple-element.19), custom_call_target="InvertDiagBlocksLowerTriangular" | custom-call | tf_op jit(solution)/shard_map/jit(_solve_triangular)/triangular_solve | solution.py:35
  668.2 4.5 convolution_bitcast_fusion.1
  673.9 73.0 %all-reduce.13.cloned.1.call-done = f32[512,256]{0,1:T(8,128)} async-done(((f32[512,256]{0,1:T(8,128)}), f32[512,256]{0,1:T(8,128)}) %all-reduce.13.cloned.1.call-update) | async-done | bytes 524304 | tf_op jit(solution)/shard_map/psum | solution.py:37
  751.3 11.9 %cholesky.282 = f32[128,128]{1,0:T(8,128)S(1)} custom-call(f32[128,128]{1,0:T(8,128)S(1)} %cholesky.352), custom_call_target="Cholesky" | custom-call | tf_op jit(solution)/shard_map/jit(cholesky)/cholesky | solution.py:43
  763.3 9.8 %custom-call.39 = f32[1,128,128]{1,2,0:T(8,128)S(1)} custom-call(f32[1,128,128]{2,1,0:T(8,128)S(1)} %get-tuple-element.87), custom_call_target="InvertDiagBlocksLowerTriangular" | custom-call | tf_op jit(solution)/shard_map/jit(cholesky)/cholesky | solution.py:43
  775.3 11.7 %cholesky.299 = f32[128,128]{1,0:T(8,128)S(1)} custom-call(f32[128,128]{1,0:T(8,128)S(1)} %convolution_subtract_fusion.7), custom_call_target="Cholesky" | custom-call | tf_op jit(solution)/shard_map/jit(cholesky)/cholesky | solution.py:43
  790.6 4.1 while.6
  795.4 20.5 %custom-call.32 = f32[2,128,128]{1,2,0:T(8,128)S(1)} custom-call(f32[2,128,128]{2,1,0:T(8,128)} %copy-done.18), custom_call_target="InvertDiagBlocksLowerTriangular" | custom-call | tf_op jit(solution)/shard_map/jit(_cho_solve)/triangular_solve | solution.py:43
  (151 shorter events, 68.2 us)
Async XLA Ops:
  7.2 1.6 copy-start
  7.2 140.8 %all-reduce.17.cloned.1.call-start = ((), (), s32[]{:S(2)}) async-start(), calls=%async_computation.4 | async-start | bytes 4194304 | tf_op jit(solution)/shard_map/psum | solution.py:28
  8.8 16.6 %copy-start.1 = (f32[1024,2048]{1,0:T(8,128)S(1)}, f32[1024,2048]{1,0:T(8,128)}, u32[]{:S(2)}) copy-start(f32[1024,2048]{1,0:T(8,128)} %param.6) | copy-start | bytes 25165828
  8.8 16.7 %copy-start.11 = (f32[2048,256]{1,0:T(8,128)S(1)}, f32[2048,256]{1,0:T(8,128)}, u32[]{:S(2)}) copy-start(f32[2048,256]{1,0:T(8,128)} %param.7) | copy-start | bytes 6291460
  25.4 7.6 copy-start.3
  41.1 111.0 %copy-start.14 = (f32[256,1024]{1,0:T(8,128)S(1)}, f32[256,1024]{1,0:T(8,128)}, u32[]{:S(2)}) copy-start(f32[256,1024]{1,0:T(8,128)} %param.8) | copy-start | bytes 3145732
  41.2 251.1 %all-reduce.9.cloned.1.call-start = ((), (), s32[]{:S(2)}) async-start(), calls=%async_computation | async-start | bytes 524288 | tf_op jit(solution)/shard_map/psum | solution.py:30
  152.1 364.6 %all-reduce.15.cloned.1.call-start = ((), (), s32[]{:S(2)}) async-start(), calls=%async_computation.3 | async-start | bytes 7340032 | tf_op jit(solution)/shard_map/psum | solution.py:29
  162.9 196.4 %copy-start.5 = (f32[1024,256]{1,0:T(8,128)S(1)}, f32[1024,256]{1,0:T(8,128)}, u32[]{:S(2)}) copy-start(f32[1024,256]{1,0:T(8,128)} %get-tuple-element.74) | copy-start | bytes 3145732
  294.4 0.7 copy-start.15
  330.6 2.0 copy-start.13
  337.7 0.7 copy-start.19
  359.9 4.4 copy-start.6
  364.4 1.0 copy-start.7
  364.4 232.3 %all-reduce.11.cloned.1.call-start = ((), (), s32[]{:S(2)}) async-start(), calls=%async_computation.1 | async-start | bytes 524288 | tf_op jit(solution)/shard_map/psum | solution.py:31
  516.7 5.1 copy-start.10
  521.6 225.4 %all-reduce.13.cloned.1.call-start = ((), (), s32[]{:S(2)}) async-start(), calls=%async_computation.2 | async-start | bytes 1048576 | tf_op jit(solution)/shard_map/psum | solution.py:37
  598.8 11.7 %copy-start.16 = (f32[256,256]{1,0:T(8,128)}, f32[256,256]{1,0:T(8,128)S(1)}, u32[]{:S(2)}) copy-start(f32[256,256]{1,0:T(8,128)S(1)} %fusion.14) | copy-start | bytes 786436
  660.8 2.4 copy-start.2
  665.3 2.9 copy-start.4
  665.5 1.3 copy-start.8
  748.8 67.1 %copy-start.9 = (f32[512,256]{0,1:T(8,128)S(1)}, f32[512,256]{0,1:T(8,128)}, u32[]{:S(2)}) copy-start(f32[512,256]{0,1:T(8,128)} %all-reduce.13.cloned.1.call-done) | copy-start | bytes 1572868
  750.6 0.7 copy-start.17
  787.0 2.6 copy-start.12
  794.8 0.7 copy-start.18
Sparse Core Ops, SparseCore 0:
  41.3 106.6 all-reduce.16
  152.2 140.0 all-reduce.8
  364.5 152.1 all-reduce.14
  521.7 74.9 all-reduce.10
  672.9 74.0 all-reduce.12
